TPU v7x, 32 devices: a whole 2x2x4 slice. The times are simulated.
32 devices in a mesh: row: 8 (over z, core), col: 4 (over y, x).
Axes of the slice: x: 2, y: 2, z: 4, core: 2. Of those that a mesh axis runs over, the one named last changes fastest.
Arguments:
- amplitudes: float32 [8, 4, 2, 65536], P('row', 'col'), may hold values from -6 to 6
- gate_real: float32 [2, 3, 128, 128], replicated, may hold values from -0.375 to 0.375
- gate_imag: float32 [2, 3, 128, 128], replicated, may hold values from -0.375 to 0.375
- gate_qubits: int32 [2, 3, 9], replicated, may hold values from 0 to 8, each once within a row
- swap_qubits: int32 [2, 9], replicated, may hold values from 0 to 8, each once within a row
Outputs:
- evolved: float32 [8, 4, 2, 65536], P('row', 'col')
Inputs may be any that keep to these rules, and one draw needn't show every extreme that they name: `gate_qubits`: each row is an ordering of 0 to 8; a gate acts on local qubits 7 + its first 7 entries, entry j giving bit j of the gate index. `swap_qubits`: each row is an ordering of 0 to 8; in a round on an axis with k index bits, local qubit 7 + entry j for j < k is swapped with bit j of that axis's index.
All inputs are finite; a program needn't handle non-finite values.
Results may differ from a plain program's by a relative error of at most 0.0001.
Values sent between devices are 32-bit elements; how exact they have to be, the bound alone decides.
No kernel may reach another device: no remote copies, remote signals or barrier semaphores. Data moves between devices by JAX's collectives and lax.ppermute only.
A program may use at most 64 MiB of HBM per device.

v0:
```python
import jax
import jax.numpy as jnp
from jax import lax
from jax.sharding import PartitionSpec as P


def spread_bits(dest, total_bits):
    low_count = total_bits // 2
    high_count = total_bits - low_count

    def table(count, offset):
        position = jnp.arange(2**count, dtype=jnp.int32)
        result = jnp.zeros_like(position)
        for bit_index in range(count):
            result = result + jnp.left_shift(position >> bit_index & 1, dest[offset + bit_index])
        return result

    low_table = table(low_count, 0)
    high_table = table(high_count, low_count)
    return (high_table[:, None] + low_table[None, :]).reshape(-1)


def qubit_maps(chosen, top_count, total_bits):
    qubits = jnp.arange(total_bits, dtype=jnp.int32)
    picked = chosen[:top_count]
    matches = picked[:, None] == qubits[None, :]
    chosen_mask = jnp.any(matches, axis=0)
    slot_top = jnp.sum(
        jnp.where(matches, jnp.arange(top_count, dtype=jnp.int32)[:, None], 0), axis=0
    )
    unchosen = jnp.where(chosen_mask, 0, 1).astype(jnp.int32)
    rest_rank = jnp.cumsum(unchosen) - unchosen
    ordering = jnp.argsort(jnp.where(chosen_mask, total_bits + qubits, qubits))
    low_bits = total_bits - top_count
    forward_dest = jnp.concatenate([ordering[:low_bits], picked])
    backward_dest = jnp.where(chosen_mask, low_bits + slot_top, rest_rank)
    return (spread_bits(forward_dest, total_bits), spread_bits(backward_dest, total_bits))


def per_device(amplitudes, gate_real, gate_imag, gate_qubits, swap_qubits):
    local_size = amplitudes.shape[-1]
    total_bits = local_size.bit_length() - 1
    gate_size = gate_real.shape[-1]
    gate_bits = gate_size.bit_length() - 1
    high_bits = total_bits - gate_bits
    row_count = local_size // gate_size
    current = amplitudes.reshape(2, row_count, gate_size)
    for round_index in range(gate_real.shape[0]):
        for gate_index in range(gate_real.shape[1]):
            forward, backward = qubit_maps(
                gate_qubits[round_index, gate_index], gate_bits, high_bits
            )
            gathered = jnp.take(current, forward, axis=1, mode="clip").reshape(
                2 * gate_size, local_size // gate_size
            )
            real_part = gate_real[round_index, gate_index]
            imag_part = gate_imag[round_index, gate_index]
            operator = jnp.concatenate(
                [
                    jnp.concatenate([real_part, -imag_part], 1),
                    jnp.concatenate([imag_part, real_part], 1),
                ],
                0,
            )
            applied = jnp.dot(
                operator,
                gathered,
                precision=lax.Precision.HIGHEST,
                preferred_element_type=jnp.float32,
            ).reshape(2, row_count, gate_size)
            current = jnp.take(applied, backward, axis=1, mode="clip")
            current = (
                current.reshape(2, row_count // gate_size, gate_size, gate_size)
                .transpose(0, 1, 3, 2)
                .reshape(2, row_count, gate_size)
            )
        if round_index % 2 == 0:
            devices = lax.axis_size("row")
            forward, backward = qubit_maps(
                swap_qubits[round_index], devices.bit_length() - 1, high_bits
            )
            prepared = jnp.take(current, forward, axis=1, mode="clip").reshape(
                2, devices, local_size // devices
            )
            arrived = lax.all_to_all(prepared, "row", split_axis=1, concat_axis=1, tiled=True)
        else:
            devices = lax.axis_size("col")
            forward, backward = qubit_maps(
                swap_qubits[round_index], devices.bit_length() - 1, high_bits
            )
            prepared = jnp.take(current, forward, axis=1, mode="clip").reshape(
                2, devices, local_size // devices
            )
            arrived = lax.all_to_all(prepared, "col", split_axis=1, concat_axis=1, tiled=True)
        current = jnp.take(arrived.reshape(2, row_count, gate_size), backward, axis=1, mode="clip")
    return current.reshape(amplitudes.shape)


def solution(mesh):
    placed = (P("row", "col", None, None), P(), P(), P(), P())
    return jax.shard_map(
        per_device,
        mesh=mesh,
        in_specs=placed,
        out_specs=P("row", "col", None, None),
        check_vma=False,
    )
```

profile of v0, /device:TPU:0, one launch (start us, length us, event | category | flops | bytes accessed | tf_op | source)
XLA Modules:
  0.0 183.7 jit_solution(13351006384527950985)
XLA Ops:
  0.0 1.7 fusion.77
  4.4 1.3 sort.115
  6.3 2.5 %shift-left_add_fusion.30 = s32[16]{0:T(128)S(1)} fusion(s32[]{:T(128)} %bitcast.22, s32[]{:T(128)} %bitcast.21, s32[]{:T(128)} %bitcast.20, s32[]{:T(128)} %bitcast.19), kind=kLoop, calls=%fused_computation.192 | loop fusion | flops 240 | bytes 80 | tf_op jit(solution)/shard_map/add | solution.py:15
  8.8 3.2 %shift-left_add_fusion.31 = s32[32]{0:T(128)S(1)} fusion(s32[]{:T(128)} %bitcast.17, s32[]{:T(128)} %bitcast.16, s32[]{:T(128)} %bitcast.15, s32[]{:T(128)} %bitcast.14, s32[]{:T(128)} %bitcast.13), kind=kLoop, calls=%fused_computation.200 | loop fusion | flops 608 | bytes 148 | tf_op jit(solution)/shard_map/add | solution.py:15
  12.1 2.1 %gather_fusion = f32[512,2,128]{2,1,0:T(2,128)S(1)} fusion(f32[2,512,128]{2,0,1:T(2,128)S(1)} %bitcast.305, s32[1024]{0:T(1024)S(1)} %pad_clamp_fusion.15), kind=kCustom, calls=%fused_computation | custom fusion | bytes 1050624 | tf_op jit(solution)/shard_map/jit(_take)/gather | solution.py:53
  14.4 0.9 copy-done.1
  15.3 1.0 copy-done.2
  17.4 0.7 fusion.94
  18.1 2.4 %shift-left_add_fusion.28 = s32[16]{0:T(128)S(1)} fusion(s32[]{:T(128)} %bitcast.34, s32[]{:T(128)} %bitcast.33, s32[]{:T(128)} %bitcast.32, s32[]{:T(128)} %bitcast.31), kind=kLoop, calls=%fused_computation.190 | loop fusion | flops 240 | bytes 80 | tf_op jit(solution)/shard_map/add | solution.py:15
  20.5 3.3 %shift-left_add_fusion.29 = s32[32]{0:T(128)S(1)} fusion(s32[]{:T(128)} %bitcast.30, s32[]{:T(128)} %bitcast.29, s32[]{:T(128)} %bitcast.28, s32[]{:T(128)} %bitcast.27, s32[]{:T(128)} %bitcast.26), kind=kLoop, calls=%fused_computation.191 | loop fusion | flops 608 | bytes 148 | tf_op jit(solution)/shard_map/add | solution.py:15
  23.9 2.1 %gather_fusion.1 = f32[512,2,128]{2,1,0:T(2,128)S(1)} fusion(f32[2,512,128]{2,0,1:T(2,128)S(1)} %copy.85, s32[1024]{0:T(1024)S(1)} %pad_clamp_fusion.14), kind=kCustom, calls=%fused_computation.1 | custom fusion | bytes 1050624 | tf_op jit(solution)/shard_map/jit(_take)/gather | solution.py:71
  26.9 1.3 sort.116
  28.8 2.5 %shift-left_add_fusion.26 = s32[16]{0:T(128)S(1)} fusion(s32[]{:T(128)} %bitcast.48, s32[]{:T(128)} %bitcast.47, s32[]{:T(128)} %bitcast.46, s32[]{:T(128)} %bitcast.45), kind=kLoop, calls=%fused_computation.186 | loop fusion | flops 240 | bytes 80 | tf_op jit(solution)/shard_map/add | solution.py:15
  31.3 3.1 %shift-left_add_fusion.27 = s32[32]{0:T(128)S(1)} fusion(s32[]{:T(128)} %bitcast.43, s32[]{:T(128)} %bitcast.42, s32[]{:T(128)} %bitcast.41, s32[]{:T(128)} %bitcast.40, s32[]{:T(128)} %bitcast.39), kind=kLoop, calls=%fused_computation.189 | loop fusion | flops 608 | bytes 148 | tf_op jit(solution)/shard_map/add | solution.py:15
  34.5 2.1 %gather_fusion.2 = f32[512,2,128]{2,1,0:T(2,128)S(1)} fusion(f32[2,512,128]{2,0,1:T(2,128)S(1)} %copy.87, s32[1024]{0:T(1024)S(1)} %pad_clamp_fusion.13), kind=kCustom, calls=%fused_computation.2 | custom fusion | bytes 1050624 | tf_op jit(solution)/shard_map/jit(_take)/gather | solution.py:53
  38.5 2.4 %shift-left_add_fusion.24 = s32[16]{0:T(128)S(1)} fusion(s32[]{:T(128)} %bitcast.60, s32[]{:T(128)} %bitcast.59, s32[]{:T(128)} %bitcast.58, s32[]{:T(128)} %bitcast.57), kind=kLoop, calls=%fused_computation.184 | loop fusion | flops 240 | bytes 80 | tf_op jit(solution)/shard_map/add | solution.py:15
  41.0 3.1 %shift-left_add_fusion.25 = s32[32]{0:T(128)S(1)} fusion(s32[]{:T(128)} %bitcast.56, s32[]{:T(128)} %bitcast.55, s32[]{:T(128)} %bitcast.54, s32[]{:T(128)} %bitcast.53, s32[]{:T(128)} %bitcast.52), kind=kLoop, calls=%fused_computation.185 | loop fusion | flops 608 | bytes 148 | tf_op jit(solution)/shard_map/add | solution.py:15
  44.3 2.1 %gather_fusion.3 = f32[512,2,128]{2,1,0:T(2,128)S(1)} fusion(f32[2,512,128]{2,0,1:T(2,128)S(1)} %copy.89, s32[1024]{0:T(1024)S(1)} %pad_clamp_fusion.12), kind=kCustom, calls=%fused_computation.3 | custom fusion | bytes 1050624 | tf_op jit(solution)/shard_map/jit(_take)/gather | solution.py:71
  47.2 1.3 sort.117
  49.0 2.5 %shift-left_add_fusion.22 = s32[16]{0:T(128)S(1)} fusion(s32[]{:T(128)} %bitcast.74, s32[]{:T(128)} %bitcast.73, s32[]{:T(128)} %bitcast.72, s32[]{:T(128)} %bitcast.71), kind=kLoop, calls=%fused_computation.180 | loop fusion | flops 240 | bytes 80 | tf_op jit(solution)/shard_map/add | solution.py:15
  51.5 3.2 %shift-left_add_fusion.23 = s32[32]{0:T(128)S(1)} fusion(s32[]{:T(128)} %bitcast.69, s32[]{:T(128)} %bitcast.68, s32[]{:T(128)} %bitcast.67, s32[]{:T(128)} %bitcast.66, s32[]{:T(128)} %bitcast.65), kind=kLoop, calls=%fused_computation.183 | loop fusion | flops 608 | bytes 148 | tf_op jit(solution)/shard_map/add | solution.py:15
  54.9 2.1 %gather_fusion.4 = f32[512,2,128]{2,1,0:T(2,128)S(1)} fusion(f32[2,512,128]{2,0,1:T(2,128)S(1)} %copy.91, s32[1024]{0:T(1024)S(1)} %pad_clamp_fusion.11), kind=kCustom, calls=%fused_computation.4 | custom fusion | bytes 1050624 | tf_op jit(solution)/shard_map/jit(_take)/gather | solution.py:53
  58.8 2.6 %shift-left_add_fusion.20 = s32[16]{0:T(128)S(1)} fusion(s32[]{:T(128)} %bitcast.86, s32[]{:T(128)} %bitcast.85, s32[]{:T(128)} %bitcast.84, s32[]{:T(128)} %bitcast.83), kind=kLoop, calls=%fused_computation.178 | loop fusion | flops 240 | bytes 80 | tf_op jit(solution)/shard_map/add | solution.py:15
  61.4 3.1 %shift-left_add_fusion.21 = s32[32]{0:T(128)S(1)} fusion(s32[]{:T(128)} %bitcast.82, s32[]{:T(128)} %bitcast.81, s32[]{:T(128)} %bitcast.80, s32[]{:T(128)} %bitcast.79, s32[]{:T(128)} %bitcast.78), kind=kLoop, calls=%fused_computation.179 | loop fusion | flops 608 | bytes 148 | tf_op jit(solution)/shard_map/add | solution.py:15
  64.7 2.1 %gather_fusion.5 = f32[512,2,128]{2,1,0:T(2,128)S(1)} fusion(f32[2,512,128]{2,0,1:T(2,128)S(1)} %copy.93, s32[1024]{0:T(1024)S(1)} %pad_clamp_fusion.10), kind=kCustom, calls=%fused_computation.5 | custom fusion | bytes 1050624 | tf_op jit(solution)/shard_map/jit(_take)/gather | solution.py:71
  67.6 1.3 sort.118
  69.5 2.5 %shift-left_add_fusion.18 = s32[16]{0:T(128)S(1)} fusion(s32[]{:T(128)} %bitcast.100, s32[]{:T(128)} %bitcast.99, s32[]{:T(128)} %bitcast.98, s32[]{:T(128)} %bitcast.97), kind=kLoop, calls=%fused_computation.174 | loop fusion | flops 240 | bytes 80 | tf_op jit(solution)/shard_map/add | solution.py:15
  72.0 3.1 %shift-left_add_fusion.19 = s32[32]{0:T(128)S(1)} fusion(s32[]{:T(128)} %bitcast.96, s32[]{:T(128)} %bitcast.95, s32[]{:T(128)} %bitcast.94, s32[]{:T(128)} %bitcast.93, s32[]{:T(128)} %bitcast.92), kind=kLoop, calls=%fused_computation.175 | loop fusion | flops 608 | bytes 148 | tf_op jit(solution)/shard_map/add | solution.py:15
  75.3 2.5 %gather_fusion.6 = f32[512,2,128]{2,1,0:T(2,128)} fusion(f32[2,512,128]{2,0,1:T(2,128)S(1)} %copy.95, s32[1024]{0:T(1024)S(1)} %pad_clamp_fusion.9), kind=kCustom, calls=%fused_computation.6 | custom fusion | bytes 1050624 | tf_op jit(solution)/shard_map/jit(_take)/gather | solution.py:82
  77.9 6.4 %all-to-all-start = ((f32[2,8,8192]{2,0,1:T(2,128)}), f32[2,8,8192]{2,0,1:T(2,128)S(1)}, u32[]{:S(2)}, u32[]{:S(2)}) async-start(f32[2,8,8192]{2,0,1:T(2,128)} %bitcast.102), calls=%async_computation | async-start | bytes 1048576 | tf_op jit(solution)/shard_map/all_to_all | solution.py:85
  84.2 0.7 fusion.76
  86.2 1.3 sort.119
  89.0 1.2 sort.120
  91.7 1.3 sort.121
  94.6 1.3 sort.122
  97.3 2.5 %shift-left_add_fusion.16 = s32[16]{0:T(128)S(1)} fusion(s32[]{:T(128)} %bitcast.114, s32[]{:T(128)} %bitcast.113, s32[]{:T(128)} %bitcast.112, s32[]{:T(128)} %bitcast.111), kind=kLoop, calls=%fused_computation.172 | loop fusion | flops 240 | bytes 80 | tf_op jit(solution)/shard_map/add | solution.py:15
  99.8 3.1 %shift-left_add_fusion.17 = s32[32]{0:T(128)S(1)} fusion(s32[]{:T(128)} %bitcast.110, s32[]{:T(128)} %bitcast.109, s32[]{:T(128)} %bitcast.108, s32[]{:T(128)} %bitcast.107, s32[]{:T(128)} %bitcast.106), kind=kLoop, calls=%fused_computation.173 | loop fusion | flops 608 | bytes 148 | tf_op jit(solution)/shard_map/add | solution.py:15
  102.9 2.5 %shift-left_add_fusion.14 = s32[16]{0:T(128)S(1)} fusion(s32[]{:T(128)} %bitcast.125, s32[]{:T(128)} %bitcast.124, s32[]{:T(128)} %bitcast.123, s32[]{:T(128)} %bitcast.122), kind=kLoop, calls=%fused_computation.168 | loop fusion | flops 240 | bytes 80 | tf_op jit(solution)/shard_map/add | solution.py:15
  105.4 3.2 %shift-left_add_fusion.15 = s32[32]{0:T(128)S(1)} fusion(s32[]{:T(128)} %bitcast.120, s32[]{:T(128)} %bitcast.119, s32[]{:T(128)} %bitcast.118, s32[]{:T(128)} %bitcast.117, s32[]{:T(128)} %bitcast.116), kind=kLoop, calls=%fused_computation.171 | loop fusion | flops 608 | bytes 148 | tf_op jit(solution)/shard_map/add | solution.py:15
  108.7 2.5 %shift-left_add_fusion.12 = s32[16]{0:T(128)S(1)} fusion(s32[]{:T(128)} %bitcast.137, s32[]{:T(128)} %bitcast.136, s32[]{:T(128)} %bitcast.135, s32[]{:T(128)} %bitcast.134), kind=kLoop, calls=%fused_computation.166 | loop fusion | flops 240 | bytes 80 | tf_op jit(solution)/shard_map/add | solution.py:15
  111.2 3.2 %shift-left_add_fusion.13 = s32[32]{0:T(128)S(1)} fusion(s32[]{:T(128)} %bitcast.133, s32[]{:T(128)} %bitcast.132, s32[]{:T(128)} %bitcast.131, s32[]{:T(128)} %bitcast.130, s32[]{:T(128)} %bitcast.129), kind=kLoop, calls=%fused_computation.167 | loop fusion | flops 608 | bytes 148 | tf_op jit(solution)/shard_map/add | solution.py:15
  114.4 2.4 %shift-left_add_fusion.10 = s32[16]{0:T(128)S(1)} fusion(s32[]{:T(128)} %bitcast.151, s32[]{:T(128)} %bitcast.150, s32[]{:T(128)} %bitcast.149, s32[]{:T(128)} %bitcast.148), kind=kLoop, calls=%fused_computation.162 | loop fusion | flops 240 | bytes 80 | tf_op jit(solution)/shard_map/add | solution.py:15
  116.8 3.2 %shift-left_add_fusion.11 = s32[32]{0:T(128)S(1)} fusion(s32[]{:T(128)} %bitcast.146, s32[]{:T(128)} %bitcast.145, s32[]{:T(128)} %bitcast.144, s32[]{:T(128)} %bitcast.143, s32[]{:T(128)} %bitcast.142), kind=kLoop, calls=%fused_computation.165 | loop fusion | flops 608 | bytes 148 | tf_op jit(solution)/shard_map/add | solution.py:15
  120.1 2.4 %shift-left_add_fusion.8 = s32[16]{0:T(128)S(1)} fusion(s32[]{:T(128)} %bitcast.163, s32[]{:T(128)} %bitcast.162, s32[]{:T(128)} %bitcast.161, s32[]{:T(128)} %bitcast.160), kind=kLoop, calls=%fused_computation.160 | loop fusion | flops 240 | bytes 80 | tf_op jit(solution)/shard_map/add | solution.py:15
  122.6 3.1 %shift-left_add_fusion.9 = s32[32]{0:T(128)S(1)} fusion(s32[]{:T(128)} %bitcast.159, s32[]{:T(128)} %bitcast.158, s32[]{:T(128)} %bitcast.157, s32[]{:T(128)} %bitcast.156, s32[]{:T(128)} %bitcast.155), kind=kLoop, calls=%fused_computation.161 | loop fusion | flops 608 | bytes 148 | tf_op jit(solution)/shard_map/add | solution.py:15
  125.7 2.6 %shift-left_add_fusion.6 = s32[16]{0:T(128)S(1)} fusion(s32[]{:T(128)} %bitcast.177, s32[]{:T(128)} %bitcast.176, s32[]{:T(128)} %bitcast.175, s32[]{:T(128)} %bitcast.174), kind=kLoop, calls=%fused_computation.156 | loop fusion | flops 240 | bytes 80 | tf_op jit(solution)/shard_map/add | solution.py:15
  128.3 3.0 %shift-left_add_fusion.7 = s32[32]{0:T(128)S(1)} fusion(s32[]{:T(128)} %bitcast.172, s32[]{:T(128)} %bitcast.171, s32[]{:T(128)} %bitcast.170, s32[]{:T(128)} %bitcast.169, s32[]{:T(128)} %bitcast.168), kind=kLoop, calls=%fused_computation.159 | loop fusion | flops 608 | bytes 148 | tf_op jit(solution)/shard_map/add | solution.py:15
  131.4 2.5 %shift-left_add_fusion.4 = s32[16]{0:T(128)S(1)} fusion(s32[]{:T(128)} %bitcast.189, s32[]{:T(128)} %bitcast.188, s32[]{:T(128)} %bitcast.187, s32[]{:T(128)} %bitcast.186), kind=kLoop, calls=%fused_computation.154 | loop fusion | flops 240 | bytes 80 | tf_op jit(solution)/shard_map/add | solution.py:15
  133.9 3.2 %shift-left_add_fusion.5 = s32[32]{0:T(128)S(1)} fusion(s32[]{:T(128)} %bitcast.185, s32[]{:T(128)} %bitcast.184, s32[]{:T(128)} %bitcast.183, s32[]{:T(128)} %bitcast.182, s32[]{:T(128)} %bitcast.181), kind=kLoop, calls=%fused_computation.155 | loop fusion | flops 608 | bytes 148 | tf_op jit(solution)/shard_map/add | solution.py:15
  137.2 2.5 %shift-left_add_fusion.2 = s32[16]{0:T(128)S(1)} fusion(s32[]{:T(128)} %bitcast.203, s32[]{:T(128)} %bitcast.202, s32[]{:T(128)} %bitcast.201, s32[]{:T(128)} %bitcast.200), kind=kLoop, calls=%fused_computation.150 | loop fusion | flops 240 | bytes 80 | tf_op jit(solution)/shard_map/add | solution.py:15
  139.7 3.1 %shift-left_add_fusion.3 = s32[32]{0:T(128)S(1)} fusion(s32[]{:T(128)} %bitcast.199, s32[]{:T(128)} %bitcast.198, s32[]{:T(128)} %bitcast.197, s32[]{:T(128)} %bitcast.196, s32[]{:T(128)} %bitcast.195), kind=kLoop, calls=%fused_computation.151 | loop fusion | flops 608 | bytes 148 | tf_op jit(solution)/shard_map/add | solution.py:15
  142.9 2.5 %shift-left_add_fusion = s32[16]{0:T(128)S(1)} fusion(s32[]{:T(128)} %bitcast.217, s32[]{:T(128)} %bitcast.216, s32[]{:T(128)} %bitcast.215, s32[]{:T(128)} %bitcast.214), kind=kLoop, calls=%fused_computation.148 | loop fusion | flops 240 | bytes 80 | tf_op jit(solution)/shard_map/add | solution.py:15
  146.2 2.1 %gather_fusion.7 = f32[512,2,128]{2,1,0:T(2,128)S(1)} fusion(f32[2,512,128]{2,0,1:T(2,128)S(1)} %bitcast.306, s32[1024]{0:T(1024)S(1)} %pad_clamp_fusion.8), kind=kCustom, calls=%fused_computation.7 | custom fusion | bytes 1050624 | tf_op jit(solution)/shard_map/jit(_take)/gather | solution.py:95
  148.3 2.1 %gather_fusion.8 = f32[512,2,128]{2,1,0:T(2,128)S(1)} fusion(f32[2,512,128]{2,0,1:T(2,128)S(1)} %bitcast.308, s32[1024]{0:T(1024)S(1)} %pad_clamp_fusion.7), kind=kCustom, calls=%fused_computation.8 | custom fusion | bytes 1050624 | tf_op jit(solution)/shard_map/jit(_take)/gather | solution.py:53
  151.6 2.1 %gather_fusion.9 = f32[512,2,128]{2,1,0:T(2,128)S(1)} fusion(f32[2,512,128]{2,0,1:T(2,128)S(1)} %copy.101, s32[1024]{0:T(1024)S(1)} %pad_clamp_fusion.6), kind=kCustom, calls=%fused_computation.9 | custom fusion | bytes 1050624 | tf_op jit(solution)/shard_map/jit(_take)/gather | solution.py:71
  154.3 2.1 %gather_fusion.10 = f32[512,2,128]{2,1,0:T(2,128)S(1)} fusion(f32[2,512,128]{2,0,1:T(2,128)S(1)} %copy.103, s32[1024]{0:T(1024)S(1)} %pad_clamp_fusion.5), kind=kCustom, calls=%fused_computation.10 | custom fusion | bytes 1050624 | tf_op jit(solution)/shard_map/jit(_take)/gather | solution.py:53
  157.6 2.1 %gather_fusion.11 = f32[512,2,128]{2,1,0:T(2,128)S(1)} fusion(f32[2,512,128]{2,0,1:T(2,128)S(1)} %copy.105, s32[1024]{0:T(1024)S(1)} %pad_clamp_fusion.4), kind=kCustom, calls=%fused_computation.11 | custom fusion | bytes 1050624 | tf_op jit(solution)/shard_map/jit(_take)/gather | solution.py:71
  160.3 2.1 %gather_fusion.12 = f32[512,2,128]{2,1,0:T(2,128)S(1)} fusion(f32[2,512,128]{2,0,1:T(2,128)S(1)} %copy.107, s32[1024]{0:T(1024)S(1)} %pad_clamp_fusion.3), kind=kCustom, calls=%fused_computation.12 | custom fusion | bytes 1050624 | tf_op jit(solution)/shard_map/jit(_take)/gather | solution.py:53
  163.6 2.1 %gather_fusion.13 = f32[512,2,128]{2,1,0:T(2,128)S(1)} fusion(f32[2,512,128]{2,0,1:T(2,128)S(1)} %copy.109, s32[1024]{0:T(1024)S(1)} %pad_clamp_fusion.2), kind=kCustom, calls=%fused_computation.13 | custom fusion | bytes 1050624 | tf_op jit(solution)/shard_map/jit(_take)/gather | solution.py:71
  166.3 2.5 %gather_fusion.14 = f32[512,2,128]{2,1,0:T(2,128)} fusion(f32[2,512,128]{2,0,1:T(2,128)S(1)} %copy.111, s32[1024]{0:T(1024)S(1)} %pad_clamp_fusion.1), kind=kCustom, calls=%fused_computation.14 | custom fusion | bytes 1050624 | tf_op jit(solution)/shard_map/jit(_take)/gather | solution.py:91
  168.8 3.7 %all-to-all-start.1 = ((f32[2,4,16384]{2,0,1:T(2,128)}), f32[2,4,16384]{2,0,1:T(2,128)S(1)}, u32[]{:S(2)}, u32[]{:S(2)}) async-start(f32[2,4,16384]{2,0,1:T(2,128)} %bitcast.205), calls=%async_computation.1 | async-start | bytes 1048576 | tf_op jit(solution)/shard_map/all_to_all | solution.py:94
  172.5 3.1 %shift-left_add_fusion.1 = s32[32]{0:T(128)S(1)} fusion(s32[]{:T(128)} %bitcast.213, s32[]{:T(128)} %bitcast.212, s32[]{:T(128)} %bitcast.211, s32[]{:T(128)} %bitcast.210, s32[]{:T(128)} %bitcast.209), kind=kLoop, calls=%fused_computation.149 | loop fusion | flops 608 | bytes 148 | tf_op jit(solution)/shard_map/add | solution.py:15
  175.7 5.5 %all-to-all-done.1 = f32[2,4,16384]{2,0,1:T(2,128)S(1)} async-done(((f32[2,4,16384]{2,0,1:T(2,128)}), f32[2,4,16384]{2,0,1:T(2,128)S(1)}, u32[]{:S(2)}, u32[]{:S(2)}) %all-to-all-start.1) | async-done | bytes 524320 | tf_op jit(solution)/shard_map/all_to_all | solution.py:94
  181.2 2.5 %gather_fusion.15 = f32[512,2,128]{2,1,0:T(2,128)} fusion(f32[2,512,128]{2,0,1:T(2,128)S(1)} %bitcast.307, s32[1024]{0:T(1024)S(1)} %pad_clamp_fusion), kind=kCustom, calls=%fused_computation.15 | custom fusion | bytes 1050624 | tf_op jit(solution)/shard_map/jit(_take)/gather | solution.py:95
  (163 shorter events, 27.5 us)
Async XLA Ops:
  0.0 12.1 %copy-start = (f32[1,1,2,65536]{3,2,1,0:T(2,128)S(1)}, f32[1,1,2,65536]{3,2,1,0:T(2,128)}, u32[]{:S(2)}) copy-start(f32[1,1,2,65536]{3,2,1,0:T(2,128)} %param.5) | copy-start | bytes 1572868
  0.0 1.7 copy-start.3
  2.7 0.7 copy-start.4
  14.3 1.0 copy-start.1
  15.3 1.0 copy-start.2
  77.9 68.3 %all-to-all-start = ((f32[2,8,8192]{2,0,1:T(2,128)}), f32[2,8,8192]{2,0,1:T(2,128)S(1)}, u32[]{:S(2)}, u32[]{:S(2)}) async-start(f32[2,8,8192]{2,0,1:T(2,128)} %bitcast.102), calls=%async_computation | async-start | bytes 1048576 | tf_op jit(solution)/shard_map/all_to_all | solution.py:85
  168.8 12.4 %all-to-all-start.1 = ((f32[2,4,16384]{2,0,1:T(2,128)}), f32[2,4,16384]{2,0,1:T(2,128)S(1)}, u32[]{:S(2)}, u32[]{:S(2)}) async-start(f32[2,4,16384]{2,0,1:T(2,128)} %bitcast.205), calls=%async_computation.1 | async-start | bytes 1048576 | tf_op jit(solution)/shard_map/all_to_all | solution.py:94
where the time goes:
time: 185 us; the launch traced here: 184 us
  other arithmetic  104 us (56%)
  local copies, waits for them, and re-layouts  59.7 us (32%)
  starting transfers between devices  10.1 us (5%)
  waiting for transfers between devices  5.47 us (3%)
  matrix products  3.62 us (2%)
    add x32, other arithmetic, table(): result + jnp.left_shift(position >> bit_index & 1, dest[offset + bit_index])  90 us
    gather x14, local copies, waits for them, and re-layouts, per_device(): jnp.take(current, forward, axis=1, mode='clip')  17.7 us
    slice x20, local copies, waits for them, and re-layouts, table(): dest[offset + bit_index]  14.3 us
    gather x6, local copies, waits for them, and re-layouts, per_device(): current = jnp.take(applied, backward, axis=1, mode='clip')  12.5 us
    sort x8, other arithmetic, qubit_maps(): ordering = jnp.argsort(jnp.where(chosen_mask, total_bits + qubits, qubits))  10.3 us
    all_to_all x1, starting transfers between devices, per_device(): lax.all_to_all(prepared, 'row', split_axis=1, concat_axis=1, tiled=True)  6.36 us
    all_to_all x1, waiting for transfers between devices, per_device(): lax.all_to_all(prepared, 'col', split_axis=1, concat_axis=1, tiled=True)  5.47 us
    gather x2, local copies, waits for them, and re-layouts, per_device(): jnp.take(arrived.reshape(2, row_count, gate_size), backward, axis=1, mode...  4.6 us
  transfers between devices with their start and end apart: 2, of which 1 were waited for; matrix products, arithmetic and copies ran while one was open for 35% of the time, Pallas kernels for 0%

commit v1 on v0

--- a/solution.py
+++ b/solution.py
@@ -82,7 +82,12 @@
             prepared = jnp.take(current, forward, axis=1, mode="clip").reshape(
                 2, devices, local_size // devices
             )
-            arrived = lax.all_to_all(prepared, "row", split_axis=1, concat_axis=1, tiled=True)
+            arrived = jnp.concatenate(
+                lax.all_to_all(
+                    jnp.stack(jnp.split(prepared, lax.axis_size("row"), axis=1)), "row", 0, 0
+                ),
+                axis=1,
+            )
         else:
             devices = lax.axis_size("col")
             forward, backward = qubit_maps(

time: 185 us -> 192 us (1.038)
  local copies, waits for them, and re-layouts: 59.7 us -> 66.1 us
    unnamed x10 -> x17, local copies, waits for them, and re-layouts: 2.46 us -> 7.24 us
    gather x14 -> x15, local copies, waits for them, and re-layouts: 17.7 us -> 17.5 us  [per_device(): jnp.take(current, forward, axis=1, mode='clip')]
  transfers between devices with their start and end apart: 2 -> 2, of which waited for: 1 -> 1; matrix products, arithmetic and copies ran while one was open for 35% -> 34% of each run, Pallas kernels for 0% -> 0%
where the time goes in v1:
time: 192 us; the launch traced here: 190 us
  other arithmetic  104 us (54%)
  local copies, waits for them, and re-layouts  66.1 us (34%)
  starting transfers between devices  10.1 us (5%)
  waiting for transfers between devices  5.42 us (3%)
  matrix products  3.62 us (2%)
    add x32, other arithmetic, table(): result + jnp.left_shift(position >> bit_index & 1, dest[offset + bit_index])  90 us
    gather x15, local copies, waits for them, and re-layouts, per_device(): jnp.take(current, forward, axis=1, mode='clip')  17.5 us
    slice x20, local copies, waits for them, and re-layouts, table(): dest[offset + bit_index]  14.3 us
    gather x6, local copies, waits for them, and re-layouts, per_device(): current = jnp.take(applied, backward, axis=1, mode='clip')  12.7 us
    sort x8, other arithmetic, qubit_maps(): ordering = jnp.argsort(jnp.where(chosen_mask, total_bits + qubits, qubits))  10.3 us
    unnamed x17, local copies, waits for them, and re-layouts  7.24 us
    all_to_all x1, starting transfers between devices, per_device(): lax.all_to_all(jnp.stack(jnp.split(prepared, lax.axis_size('row'), axis=1...  6.35 us
    all_to_all x1, waiting for transfers between devices, per_device(): lax.all_to_all(prepared, 'col', split_axis=1, concat_axis=1, tiled=True)  5.42 us
  transfers between devices with their start and end apart: 2, of which 1 were waited for; matrix products, arithmetic and copies ran while one was open for 34% of the time, Pallas kernels for 0%

profile of v1, /device:TPU:0, one launch (start us, length us, event | category | flops | bytes accessed | tf_op | source)
XLA Modules:
  0.0 190.1 jit_solution(3352906829755794238)
XLA Ops:
  0.0 1.7 fusion.85
  4.4 1.3 sort.115
  6.3 2.5 %shift-left_add_fusion.30 = s32[16]{0:T(128)S(1)} fusion(s32[]{:T(128)} %bitcast.22, s32[]{:T(128)} %bitcast.21, s32[]{:T(128)} %bitcast.20, s32[]{:T(128)} %bitcast.19), kind=kLoop, calls=%fused_computation.208 | loop fusion | flops 240 | bytes 80 | tf_op jit(solution)/shard_map/add | solution.py:15
  8.8 3.2 %shift-left_add_fusion.31 = s32[32]{0:T(128)S(1)} fusion(s32[]{:T(128)} %bitcast.17, s32[]{:T(128)} %bitcast.16, s32[]{:T(128)} %bitcast.15, s32[]{:T(128)} %bitcast.14, s32[]{:T(128)} %bitcast.13), kind=kLoop, calls=%fused_computation.216 | loop fusion | flops 608 | bytes 148 | tf_op jit(solution)/shard_map/add | solution.py:15
  12.2 2.1 %gather_fusion = f32[512,2,128]{2,1,0:T(2,128)S(1)} fusion(f32[2,512,128]{2,0,1:T(2,128)S(1)} %bitcast.339, s32[1024]{0:T(1024)S(1)} %pad_clamp_fusion.15), kind=kCustom, calls=%fused_computation | custom fusion | bytes 1050624 | tf_op jit(solution)/shard_map/jit(_take)/gather | solution.py:53
  14.4 0.9 copy-done.1
  15.3 1.0 copy-done.2
  18.1 2.4 %shift-left_add_fusion.28 = s32[16]{0:T(128)S(1)} fusion(s32[]{:T(128)} %bitcast.34, s32[]{:T(128)} %bitcast.33, s32[]{:T(128)} %bitcast.32, s32[]{:T(128)} %bitcast.31), kind=kLoop, calls=%fused_computation.206 | loop fusion | flops 240 | bytes 80 | tf_op jit(solution)/shard_map/add | solution.py:15
  20.6 3.3 %shift-left_add_fusion.29 = s32[32]{0:T(128)S(1)} fusion(s32[]{:T(128)} %bitcast.30, s32[]{:T(128)} %bitcast.29, s32[]{:T(128)} %bitcast.28, s32[]{:T(128)} %bitcast.27, s32[]{:T(128)} %bitcast.26), kind=kLoop, calls=%fused_computation.207 | loop fusion | flops 608 | bytes 148 | tf_op jit(solution)/shard_map/add | solution.py:15
  24.0 2.1 %gather_fusion.1 = f32[512,2,128]{2,1,0:T(2,128)S(1)} fusion(f32[2,512,128]{2,0,1:T(2,128)S(1)} %copy.93, s32[1024]{0:T(1024)S(1)} %pad_clamp_fusion.14), kind=kCustom, calls=%fused_computation.1 | custom fusion | bytes 1050624 | tf_op jit(solution)/shard_map/jit(_take)/gather | solution.py:71
  26.9 1.3 sort.116
  28.8 2.5 %shift-left_add_fusion.26 = s32[16]{0:T(128)S(1)} fusion(s32[]{:T(128)} %bitcast.48, s32[]{:T(128)} %bitcast.47, s32[]{:T(128)} %bitcast.46, s32[]{:T(128)} %bitcast.45), kind=kLoop, calls=%fused_computation.202 | loop fusion | flops 240 | bytes 80 | tf_op jit(solution)/shard_map/add | solution.py:15
  31.3 3.1 %shift-left_add_fusion.27 = s32[32]{0:T(128)S(1)} fusion(s32[]{:T(128)} %bitcast.43, s32[]{:T(128)} %bitcast.42, s32[]{:T(128)} %bitcast.41, s32[]{:T(128)} %bitcast.40, s32[]{:T(128)} %bitcast.39), kind=kLoop, calls=%fused_computation.205 | loop fusion | flops 608 | bytes 148 | tf_op jit(solution)/shard_map/add | solution.py:15
  34.6 2.1 %gather_fusion.2 = f32[512,2,128]{2,1,0:T(2,128)S(1)} fusion(f32[2,512,128]{2,0,1:T(2,128)S(1)} %copy.95, s32[1024]{0:T(1024)S(1)} %pad_clamp_fusion.13), kind=kCustom, calls=%fused_computation.2 | custom fusion | bytes 1050624 | tf_op jit(solution)/shard_map/jit(_take)/gather | solution.py:53
  38.5 2.4 %shift-left_add_fusion.24 = s32[16]{0:T(128)S(1)} fusion(s32[]{:T(128)} %bitcast.60, s32[]{:T(128)} %bitcast.59, s32[]{:T(128)} %bitcast.58, s32[]{:T(128)} %bitcast.57), kind=kLoop, calls=%fused_computation.200 | loop fusion | flops 240 | bytes 80 | tf_op jit(solution)/shard_map/add | solution.py:15
  41.0 3.1 %shift-left_add_fusion.25 = s32[32]{0:T(128)S(1)} fusion(s32[]{:T(128)} %bitcast.56, s32[]{:T(128)} %bitcast.55, s32[]{:T(128)} %bitcast.54, s32[]{:T(128)} %bitcast.53, s32[]{:T(128)} %bitcast.52), kind=kLoop, calls=%fused_computation.201 | loop fusion | flops 608 | bytes 148 | tf_op jit(solution)/shard_map/add | solution.py:15
  44.3 2.1 %gather_fusion.3 = f32[512,2,128]{2,1,0:T(2,128)S(1)} fusion(f32[2,512,128]{2,0,1:T(2,128)S(1)} %copy.97, s32[1024]{0:T(1024)S(1)} %pad_clamp_fusion.12), kind=kCustom, calls=%fused_computation.3 | custom fusion | bytes 1050624 | tf_op jit(solution)/shard_map/jit(_take)/gather | solution.py:71
  47.2 1.3 sort.117
  49.1 2.5 %shift-left_add_fusion.22 = s32[16]{0:T(128)S(1)} fusion(s32[]{:T(128)} %bitcast.74, s32[]{:T(128)} %bitcast.73, s32[]{:T(128)} %bitcast.72, s32[]{:T(128)} %bitcast.71), kind=kLoop, calls=%fused_computation.196 | loop fusion | flops 240 | bytes 80 | tf_op jit(solution)/shard_map/add | solution.py:15
  51.5 3.2 %shift-left_add_fusion.23 = s32[32]{0:T(128)S(1)} fusion(s32[]{:T(128)} %bitcast.69, s32[]{:T(128)} %bitcast.68, s32[]{:T(128)} %bitcast.67, s32[]{:T(128)} %bitcast.66, s32[]{:T(128)} %bitcast.65), kind=kLoop, calls=%fused_computation.199 | loop fusion | flops 608 | bytes 148 | tf_op jit(solution)/shard_map/add | solution.py:15
  54.9 2.1 %gather_fusion.4 = f32[512,2,128]{2,1,0:T(2,128)S(1)} fusion(f32[2,512,128]{2,0,1:T(2,128)S(1)} %copy.99, s32[1024]{0:T(1024)S(1)} %pad_clamp_fusion.11), kind=kCustom, calls=%fused_computation.4 | custom fusion | bytes 1050624 | tf_op jit(solution)/shard_map/jit(_take)/gather | solution.py:53
  58.9 2.6 %shift-left_add_fusion.20 = s32[16]{0:T(128)S(1)} fusion(s32[]{:T(128)} %bitcast.86, s32[]{:T(128)} %bitcast.85, s32[]{:T(128)} %bitcast.84, s32[]{:T(128)} %bitcast.83), kind=kLoop, calls=%fused_computation.194 | loop fusion | flops 240 | bytes 80 | tf_op jit(solution)/shard_map/add | solution.py:15
  61.4 3.1 %shift-left_add_fusion.21 = s32[32]{0:T(128)S(1)} fusion(s32[]{:T(128)} %bitcast.82, s32[]{:T(128)} %bitcast.81, s32[]{:T(128)} %bitcast.80, s32[]{:T(128)} %bitcast.79, s32[]{:T(128)} %bitcast.78), kind=kLoop, calls=%fused_computation.195 | loop fusion | flops 608 | bytes 148 | tf_op jit(solution)/shard_map/add | solution.py:15
  64.7 2.1 %gather_fusion.5 = f32[512,2,128]{2,1,0:T(2,128)S(1)} fusion(f32[2,512,128]{2,0,1:T(2,128)S(1)} %copy.101, s32[1024]{0:T(1024)S(1)} %pad_clamp_fusion.10), kind=kCustom, calls=%fused_computation.5 | custom fusion | bytes 1050624 | tf_op jit(solution)/shard_map/jit(_take)/gather | solution.py:71
  67.6 1.3 sort.118
  69.6 2.5 %shift-left_add_fusion.18 = s32[16]{0:T(128)S(1)} fusion(s32[]{:T(128)} %bitcast.100, s32[]{:T(128)} %bitcast.99, s32[]{:T(128)} %bitcast.98, s32[]{:T(128)} %bitcast.97), kind=kLoop, calls=%fused_computation.190 | loop fusion | flops 240 | bytes 80 | tf_op jit(solution)/shard_map/add | solution.py:15
  72.1 3.1 %shift-left_add_fusion.19 = s32[32]{0:T(128)S(1)} fusion(s32[]{:T(128)} %bitcast.96, s32[]{:T(128)} %bitcast.95, s32[]{:T(128)} %bitcast.94, s32[]{:T(128)} %bitcast.93, s32[]{:T(128)} %bitcast.92), kind=kLoop, calls=%fused_computation.191 | loop fusion | flops 608 | bytes 148 | tf_op jit(solution)/shard_map/add | solution.py:15
  75.4 2.3 %gather_fusion.6 = f32[512,2,128]{2,1,0:T(2,128)S(1)} fusion(f32[2,512,128]{2,0,1:T(2,128)S(1)} %copy.103, s32[1024]{0:T(1024)S(1)} %pad_clamp_fusion.9), kind=kCustom, calls=%fused_computation.6 | custom fusion | bytes 1050624 | tf_op jit(solution)/shard_map/jit(_take)/gather | solution.py:82
  83.3 6.4 %all-to-all-start = ((f32[8,2,1,8192]{3,2,1,0:T(1,128)}), f32[8,2,1,8192]{3,2,1,0:T(1,128)S(1)}, u32[]{:S(2)}, u32[]{:S(2)}) async-start(f32[8,2,1,8192]{3,2,1,0:T(1,128)} %fusion.48), calls=%async_computation | async-start | bytes 1048576 | tf_op jit(solution)/shard_map/all_to_all | solution.py:86
  89.8 0.7 fusion.84
  90.9 1.3 sort.122
  93.7 1.3 sort.119
  96.5 1.3 sort.120
  99.4 1.3 sort.121
  102.0 2.5 %shift-left_add_fusion.2 = s32[16]{0:T(128)S(1)} fusion(s32[]{:T(128)} %bitcast.210, s32[]{:T(128)} %bitcast.209, s32[]{:T(128)} %bitcast.208, s32[]{:T(128)} %bitcast.207), kind=kLoop, calls=%fused_computation.166 | loop fusion | flops 240 | bytes 80 | tf_op jit(solution)/shard_map/add | solution.py:15
  104.5 3.1 %shift-left_add_fusion.3 = s32[32]{0:T(128)S(1)} fusion(s32[]{:T(128)} %bitcast.206, s32[]{:T(128)} %bitcast.205, s32[]{:T(128)} %bitcast.204, s32[]{:T(128)} %bitcast.203, s32[]{:T(128)} %bitcast.202), kind=kLoop, calls=%fused_computation.167 | loop fusion | flops 608 | bytes 148 | tf_op jit(solution)/shard_map/add | solution.py:15
  107.7 2.5 %shift-left_add_fusion.16 = s32[16]{0:T(128)S(1)} fusion(s32[]{:T(128)} %bitcast.121, s32[]{:T(128)} %bitcast.120, s32[]{:T(128)} %bitcast.119, s32[]{:T(128)} %bitcast.118), kind=kLoop, calls=%fused_computation.188 | loop fusion | flops 240 | bytes 80 | tf_op jit(solution)/shard_map/add | solution.py:15
  110.1 3.2 %shift-left_add_fusion.17 = s32[32]{0:T(128)S(1)} fusion(s32[]{:T(128)} %bitcast.117, s32[]{:T(128)} %bitcast.116, s32[]{:T(128)} %bitcast.115, s32[]{:T(128)} %bitcast.114, s32[]{:T(128)} %bitcast.113), kind=kLoop, calls=%fused_computation.189 | loop fusion | flops 608 | bytes 148 | tf_op jit(solution)/shard_map/add | solution.py:15
  113.4 2.5 %shift-left_add_fusion.14 = s32[16]{0:T(128)S(1)} fusion(s32[]{:T(128)} %bitcast.132, s32[]{:T(128)} %bitcast.131, s32[]{:T(128)} %bitcast.130, s32[]{:T(128)} %bitcast.129), kind=kLoop, calls=%fused_computation.184 | loop fusion | flops 240 | bytes 80 | tf_op jit(solution)/shard_map/add | solution.py:15
  115.9 3.2 %shift-left_add_fusion.15 = s32[32]{0:T(128)S(1)} fusion(s32[]{:T(128)} %bitcast.127, s32[]{:T(128)} %bitcast.126, s32[]{:T(128)} %bitcast.125, s32[]{:T(128)} %bitcast.124, s32[]{:T(128)} %bitcast.123), kind=kLoop, calls=%fused_computation.187 | loop fusion | flops 608 | bytes 148 | tf_op jit(solution)/shard_map/add | solution.py:15
  119.1 2.5 %shift-left_add_fusion.12 = s32[16]{0:T(128)S(1)} fusion(s32[]{:T(128)} %bitcast.144, s32[]{:T(128)} %bitcast.143, s32[]{:T(128)} %bitcast.142, s32[]{:T(128)} %bitcast.141), kind=kLoop, calls=%fused_computation.182 | loop fusion | flops 240 | bytes 80 | tf_op jit(solution)/shard_map/add | solution.py:15
  121.6 3.0 %shift-left_add_fusion.13 = s32[32]{0:T(128)S(1)} fusion(s32[]{:T(128)} %bitcast.140, s32[]{:T(128)} %bitcast.139, s32[]{:T(128)} %bitcast.138, s32[]{:T(128)} %bitcast.137, s32[]{:T(128)} %bitcast.136), kind=kLoop, calls=%fused_computation.183 | loop fusion | flops 608 | bytes 148 | tf_op jit(solution)/shard_map/add | solution.py:15
  124.7 2.5 %shift-left_add_fusion.10 = s32[16]{0:T(128)S(1)} fusion(s32[]{:T(128)} %bitcast.158, s32[]{:T(128)} %bitcast.157, s32[]{:T(128)} %bitcast.156, s32[]{:T(128)} %bitcast.155), kind=kLoop, calls=%fused_computation.178 | loop fusion | flops 240 | bytes 80 | tf_op jit(solution)/shard_map/add | solution.py:15
  127.1 3.2 %shift-left_add_fusion.11 = s32[32]{0:T(128)S(1)} fusion(s32[]{:T(128)} %bitcast.153, s32[]{:T(128)} %bitcast.152, s32[]{:T(128)} %bitcast.151, s32[]{:T(128)} %bitcast.150, s32[]{:T(128)} %bitcast.149), kind=kLoop, calls=%fused_computation.181 | loop fusion | flops 608 | bytes 148 | tf_op jit(solution)/shard_map/add | solution.py:15
  130.4 2.4 %shift-left_add_fusion.8 = s32[16]{0:T(128)S(1)} fusion(s32[]{:T(128)} %bitcast.170, s32[]{:T(128)} %bitcast.169, s32[]{:T(128)} %bitcast.168, s32[]{:T(128)} %bitcast.167), kind=kLoop, calls=%fused_computation.176 | loop fusion | flops 240 | bytes 80 | tf_op jit(solution)/shard_map/add | solution.py:15
  132.8 3.2 %shift-left_add_fusion.9 = s32[32]{0:T(128)S(1)} fusion(s32[]{:T(128)} %bitcast.166, s32[]{:T(128)} %bitcast.165, s32[]{:T(128)} %bitcast.164, s32[]{:T(128)} %bitcast.163, s32[]{:T(128)} %bitcast.162), kind=kLoop, calls=%fused_computation.177 | loop fusion | flops 608 | bytes 148 | tf_op jit(solution)/shard_map/add | solution.py:15
  136.1 2.5 %shift-left_add_fusion.6 = s32[16]{0:T(128)S(1)} fusion(s32[]{:T(128)} %bitcast.184, s32[]{:T(128)} %bitcast.183, s32[]{:T(128)} %bitcast.182, s32[]{:T(128)} %bitcast.181), kind=kLoop, calls=%fused_computation.172 | loop fusion | flops 240 | bytes 80 | tf_op jit(solution)/shard_map/add | solution.py:15
  138.6 3.0 %shift-left_add_fusion.7 = s32[32]{0:T(128)S(1)} fusion(s32[]{:T(128)} %bitcast.179, s32[]{:T(128)} %bitcast.178, s32[]{:T(128)} %bitcast.177, s32[]{:T(128)} %bitcast.176, s32[]{:T(128)} %bitcast.175), kind=kLoop, calls=%fused_computation.175 | loop fusion | flops 608 | bytes 148 | tf_op jit(solution)/shard_map/add | solution.py:15
  141.7 2.5 %shift-left_add_fusion.4 = s32[16]{0:T(128)S(1)} fusion(s32[]{:T(128)} %bitcast.196, s32[]{:T(128)} %bitcast.195, s32[]{:T(128)} %bitcast.194, s32[]{:T(128)} %bitcast.193), kind=kLoop, calls=%fused_computation.170 | loop fusion | flops 240 | bytes 80 | tf_op jit(solution)/shard_map/add | solution.py:15
  144.3 3.2 %shift-left_add_fusion.5 = s32[32]{0:T(128)S(1)} fusion(s32[]{:T(128)} %bitcast.192, s32[]{:T(128)} %bitcast.191, s32[]{:T(128)} %bitcast.190, s32[]{:T(128)} %bitcast.189, s32[]{:T(128)} %bitcast.188), kind=kLoop, calls=%fused_computation.171 | loop fusion | flops 608 | bytes 148 | tf_op jit(solution)/shard_map/add | solution.py:15
  147.6 0.7 fusion.88
  148.9 2.4 %shift-left_add_fusion = s32[16]{0:T(128)S(1)} fusion(s32[]{:T(128)} %bitcast.224, s32[]{:T(128)} %bitcast.223, s32[]{:T(128)} %bitcast.222, s32[]{:T(128)} %bitcast.221), kind=kLoop, calls=%fused_computation.164 | loop fusion | flops 240 | bytes 80 | tf_op jit(solution)/shard_map/add | solution.py:15
  152.3 2.1 %gather_fusion.7 = f32[512,2,128]{2,1,0:T(2,128)S(1)} fusion(f32[2,512,128]{2,0,1:T(2,128)S(1)} %copy.106, s32[1024]{0:T(1024)S(1)} %get-tuple-element.218), kind=kCustom, calls=%fused_computation.7 | custom fusion | bytes 1050624 | tf_op jit(solution)/shard_map/jit(_take)/gather | solution.py:100
  154.4 2.1 %gather_fusion.8 = f32[512,2,128]{2,1,0:T(2,128)S(1)} fusion(f32[2,512,128]{2,0,1:T(2,128)S(1)} %bitcast.342, s32[1024]{0:T(1024)S(1)} %pad_clamp_fusion.7), kind=kCustom, calls=%fused_computation.8 | custom fusion | bytes 1050624 | tf_op jit(solution)/shard_map/jit(_take)/gather | solution.py:53
  157.7 2.1 %gather_fusion.9 = f32[512,2,128]{2,1,0:T(2,128)S(1)} fusion(f32[2,512,128]{2,0,1:T(2,128)S(1)} %copy.108, s32[1024]{0:T(1024)S(1)} %pad_clamp_fusion.6), kind=kCustom, calls=%fused_computation.9 | custom fusion | bytes 1050624 | tf_op jit(solution)/shard_map/jit(_take)/gather | solution.py:71
  160.4 2.1 %gather_fusion.10 = f32[512,2,128]{2,1,0:T(2,128)S(1)} fusion(f32[2,512,128]{2,0,1:T(2,128)S(1)} %copy.110, s32[1024]{0:T(1024)S(1)} %pad_clamp_fusion.5), kind=kCustom, calls=%fused_computation.10 | custom fusion | bytes 1050624 | tf_op jit(solution)/shard_map/jit(_take)/gather | solution.py:53
  163.7 2.1 %gather_fusion.11 = f32[512,2,128]{2,1,0:T(2,128)S(1)} fusion(f32[2,512,128]{2,0,1:T(2,128)S(1)} %copy.112, s32[1024]{0:T(1024)S(1)} %pad_clamp_fusion.4), kind=kCustom, calls=%fused_computation.11 | custom fusion | bytes 1050624 | tf_op jit(solution)/shard_map/jit(_take)/gather | solution.py:71
  166.4 2.1 %gather_fusion.12 = f32[512,2,128]{2,1,0:T(2,128)S(1)} fusion(f32[2,512,128]{2,0,1:T(2,128)S(1)} %copy.114, s32[1024]{0:T(1024)S(1)} %pad_clamp_fusion.3), kind=kCustom, calls=%fused_computation.12 | custom fusion | bytes 1050624 | tf_op jit(solution)/shard_map/jit(_take)/gather | solution.py:53
  169.6 2.3 %gather_fusion.13 = f32[512,2,128]{2,1,0:T(2,128)S(1)} fusion(f32[2,512,128]{2,0,1:T(2,128)S(1)} %copy.116, s32[1024]{0:T(1024)S(1)} %pad_clamp_fusion.2), kind=kCustom, calls=%fused_computation.13 | custom fusion | bytes 1050624 | tf_op jit(solution)/shard_map/jit(_take)/gather | solution.py:71
  172.6 2.5 %gather_fusion.14 = f32[512,2,128]{2,1,0:T(2,128)} fusion(f32[2,512,128]{2,0,1:T(2,128)S(1)} %copy.118, s32[1024]{0:T(1024)S(1)} %get-tuple-element.217), kind=kCustom, calls=%fused_computation.14 | custom fusion | bytes 1050624 | tf_op jit(solution)/shard_map/jit(_take)/gather | solution.py:96
  175.1 3.7 %all-to-all-start.1 = ((f32[2,4,16384]{2,0,1:T(2,128)}), f32[2,4,16384]{2,0,1:T(2,128)S(1)}, u32[]{:S(2)}, u32[]{:S(2)}) async-start(f32[2,4,16384]{2,0,1:T(2,128)} %bitcast.212), calls=%async_computation.1 | async-start | bytes 1048576 | tf_op jit(solution)/shard_map/all_to_all | solution.py:99
  178.8 3.1 %shift-left_add_fusion.1 = s32[32]{0:T(128)S(1)} fusion(s32[]{:T(128)} %bitcast.220, s32[]{:T(128)} %bitcast.219, s32[]{:T(128)} %bitcast.218, s32[]{:T(128)} %bitcast.217, s32[]{:T(128)} %bitcast.216), kind=kLoop, calls=%fused_computation.165 | loop fusion | flops 608 | bytes 148 | tf_op jit(solution)/shard_map/add | solution.py:15
  182.1 5.4 %all-to-all-done.1 = f32[2,4,16384]{2,0,1:T(2,128)S(1)} async-done(((f32[2,4,16384]{2,0,1:T(2,128)}), f32[2,4,16384]{2,0,1:T(2,128)S(1)}, u32[]{:S(2)}, u32[]{:S(2)}) %all-to-all-start.1) | async-done | bytes 524320 | tf_op jit(solution)/shard_map/all_to_all | solution.py:99
  187.5 2.5 %gather_fusion.15 = f32[512,2,128]{2,1,0:T(2,128)} fusion(f32[2,512,128]{2,0,1:T(2,128)S(1)} %bitcast.341, s32[1024]{0:T(1024)S(1)} %pad_clamp_fusion), kind=kCustom, calls=%fused_computation.15 | custom fusion | bytes 1050624 | tf_op jit(solution)/shard_map/jit(_take)/gather | solution.py:100
  (175 shorter events, 34.0 us)
Async XLA Ops:
  0.0 12.2 %copy-start = (f32[1,1,2,65536]{3,2,1,0:T(2,128)S(1)}, f32[1,1,2,65536]{3,2,1,0:T(2,128)}, u32[]{:S(2)}) copy-start(f32[1,1,2,65536]{3,2,1,0:T(2,128)} %param.5) | copy-start | bytes 1572868
  0.0 1.7 copy-start.3
  2.7 0.7 copy-start.4
  14.3 1.0 copy-start.1
  15.3 1.0 copy-start.2
  83.3 68.2 %all-to-all-start = ((f32[8,2,1,8192]{3,2,1,0:T(1,128)}), f32[8,2,1,8192]{3,2,1,0:T(1,128)S(1)}, u32[]{:S(2)}, u32[]{:S(2)}) async-start(f32[8,2,1,8192]{3,2,1,0:T(1,128)} %fusion.48), calls=%async_computation | async-start | bytes 1048576 | tf_op jit(solution)/shard_map/all_to_all | solution.py:86
  175.1 12.4 %all-to-all-start.1 = ((f32[2,4,16384]{2,0,1:T(2,128)}), f32[2,4,16384]{2,0,1:T(2,128)S(1)}, u32[]{:S(2)}, u32[]{:S(2)}) async-start(f32[2,4,16384]{2,0,1:T(2,128)} %bitcast.212), calls=%async_computation.1 | async-start | bytes 1048576 | tf_op jit(solution)/shard_map/all_to_all | solution.py:99
